TPU v7x, 32 devices: a whole 2x2x4 slice. The times are simulated.
32 devices in a mesh: dp: 8 (over z, x), shard: 4 (over y, core).
Axes of the slice: x: 2, y: 2, z: 4, core: 2. Of those that a mesh axis runs over, the one named last changes fastest.
Arguments:
- tokens: bfloat16 [8192, 2048], P('dp'), may hold values from -6 to 6
- block_ids: int32 [8, 1024], P('dp'), may hold values from 0 to 7, never falling along the last dimension, each value on 1 to 256 neighbouring positions
- cotangent: bfloat16 [8192, 2048], P('dp'), may hold values from -12 to 12
- gain_first: float32 [2048], P('dp'), may hold values from 0.3 to 2.5
- w_query: float32 [2048, 2048], P('dp', 'shard'), may hold values from -0.125 to 0.125
- w_key: float32 [2048, 512], P('dp', 'shard'), may hold values from -0.125 to 0.125
- w_value: float32 [2048, 512], P('dp', 'shard'), may hold values from -0.125 to 0.125
- w_output: float32 [2048, 2048], P('shard', 'dp'), may hold values from -2 to 2
- gain_second: float32 [2048], P('dp'), may hold values from 0.3 to 2.5
- w_gate: float32 [2048, 8192], P('dp', 'shard'), may hold values from -0.125 to 0.125
- w_up: float32 [2048, 8192], P('dp', 'shard'), may hold values from -0.125 to 0.125
- w_down: float32 [8192, 2048], P('shard', 'dp'), may hold values from -0.0625 to 0.0625
- moment_first: float32 [2048], P('dp'), may hold values from -6 to 6
- moment_query: float32 [2048, 2048], P('dp', 'shard'), may hold values from -4 to 4
- moment_key: float32 [2048, 512], P('dp', 'shard'), may hold values from -4 to 4
- moment_value: float32 [2048, 512], P('dp', 'shard'), may hold values from -4 to 4
- moment_output: float32 [2048, 2048], P('shard', 'dp'), may hold values from -4 to 4
- moment_second: float32 [2048], P('dp'), may hold values from -6 to 6
- moment_gate: float32 [2048, 8192], P('dp', 'shard'), may hold values from -4 to 4
- moment_up: float32 [2048, 8192], P('dp', 'shard'), may hold values from -4 to 4
- moment_down: float32 [8192, 2048], P('shard', 'dp'), may hold values from -4 to 4
- step: int32 [], replicated, may hold values from 1000 to 1999
- rate: float32 [], replicated, may hold values from 0.6 to 1.2
Outputs:
- output: bfloat16 [8192, 2048], P('dp')
- input_grad: float32 [8192, 2048], P('dp')
- global_norm: float32 [], replicated
- momentum_first: float32 [2048], P('dp')
- momentum_query: float32 [2048, 2048], P('dp', 'shard')
- momentum_key: float32 [2048, 512], P('dp', 'shard')
- momentum_value: float32 [2048, 512], P('dp', 'shard')
- momentum_output: float32 [2048, 2048], P('shard', 'dp')
- momentum_second: float32 [2048], P('dp')
- momentum_gate: float32 [2048, 8192], P('dp', 'shard')
- momentum_up: float32 [2048, 8192], P('dp', 'shard')
- momentum_down: float32 [8192, 2048], P('shard', 'dp')
- updated_first: float32 [2048], P('dp')
- updated_query: float32 [2048, 2048], P('dp', 'shard')
- updated_key: float32 [2048, 512], P('dp', 'shard')
- updated_value: float32 [2048, 512], P('dp', 'shard')
- updated_output: float32 [2048, 2048], P('shard', 'dp')
- updated_second: float32 [2048], P('dp')
- updated_gate: float32 [2048, 8192], P('dp', 'shard')
- updated_up: float32 [2048, 8192], P('dp', 'shard')
- updated_down: float32 [8192, 2048], P('shard', 'dp')
Inputs may be any that keep to these rules, and one draw needn't show every extreme that they name: `block_ids`: along each row the block numbers never fall, every number 0 to 7 appears, and a block holds 1 to 256 positions.
All inputs are finite; a program needn't handle non-finite values.
Results may differ from a plain program's by a relative error of at most 0.02.
Values may be sent and summed in bfloat16 or wider, within the bound.
A program may use at most 256 MiB of HBM per device.

v0:
```python
import math
import jax
import jax.numpy as jnp
from jax import lax
from jax.sharding import PartitionSpec as P

H = 32
KV = 8
HD = 64
CLIP = 4096
WARMUP = 2000
EPS = 1e-05
THETA = 10000000.0
NEGATIVE = -1e30


def inverse_rms(values):
    return lax.rsqrt(jnp.mean(values * values, axis=1, keepdims=True) + EPS)


def norm_back(values, inverse, gain, grad_normed):
    scaled = grad_normed * gain[None, :]
    gain_grad = jnp.sum(grad_normed * values * inverse, axis=0)
    grad_values = inverse * scaled - values * inverse**3 * jnp.mean(
        scaled * values, axis=1, keepdims=True
    )
    return (gain_grad, grad_values)


def angle_table(count, length):
    positions = (jnp.arange(count, dtype=jnp.int32) % length).astype(jnp.float32)
    powers = -2.0 * jnp.arange(HD // 2, dtype=jnp.float32) / HD
    angles = positions[:, None] * jnp.power(THETA, powers)[None, :]
    return (jnp.cos(angles)[:, None, :], jnp.sin(angles)[:, None, :])


def rotate(values, cosine, sine):
    half = values.shape[-1] // 2
    first = values[..., :half]
    second = values[..., half:]
    return jnp.concatenate(
        [first * cosine - second * sine, second * cosine + first * sine], axis=-1
    )


def unrotate(grads, cosine, sine):
    half = grads.shape[-1] // 2
    first = grads[..., :half]
    second = grads[..., half:]
    return jnp.concatenate(
        [first * cosine + second * sine, second * cosine - first * sine], axis=-1
    )


def to_items(values, seqs, length):
    shaped = values.reshape((seqs, length) + values.shape[1:])
    moved = jnp.moveaxis(shaped, 2, 1)
    return moved.reshape((seqs * values.shape[1], length) + values.shape[2:])


def from_items(items, seqs):
    groups = items.shape[0] // seqs
    shaped = items.reshape((seqs, groups) + items.shape[1:])
    moved = jnp.moveaxis(shaped, 1, 2)
    return moved.reshape((seqs * items.shape[1], groups) + items.shape[2:])


def item_scores(query, key, blocks, scale):
    scores = jnp.einsum("qgd,jd->gqj", query, key, preferred_element_type=jnp.float32) * scale
    allowed = blocks[None, :] <= blocks[:, None]
    return jnp.where(allowed[None], scores, NEGATIVE)


def attend_forward(scale):

    def run(parts):
        query, key, value, blocks = parts
        scores = item_scores(query, key, blocks, scale)
        peak = jnp.max(scores, axis=2, keepdims=True)
        weights = jnp.exp(scores - peak)
        total = jnp.sum(weights, axis=2, keepdims=True)
        probs = (weights / total).astype(jnp.bfloat16)
        mixed = jnp.einsum("gqj,jd->qgd", probs, value, preferred_element_type=jnp.float32)
        return (mixed.astype(jnp.bfloat16), peak, total)

    return run


def attend_backward(scale):

    def run(parts):
        query, key, value, blocks, peak, total, grad_mixed = parts
        scores = item_scores(query, key, blocks, scale)
        probs = jnp.exp(scores - peak) / total
        probs_low = probs.astype(jnp.bfloat16)
        grad_value = jnp.einsum(
            "gqj,qgd->jd", probs_low, grad_mixed, preferred_element_type=jnp.float32
        )
        grad_probs = jnp.einsum(
            "qgd,jd->gqj", grad_mixed, value, preferred_element_type=jnp.float32
        )
        grad_scores = (
            probs * (grad_probs - jnp.sum(probs * grad_probs, axis=2, keepdims=True))
        ).astype(jnp.bfloat16)
        grad_query = (
            jnp.einsum("gqj,jd->qgd", grad_scores, key, preferred_element_type=jnp.float32) * scale
        )
        grad_key = (
            jnp.einsum("gqj,qgd->jd", grad_scores, query, preferred_element_type=jnp.float32)
            * scale
        )
        return (grad_query, grad_key, grad_value)

    return run


def on_device(
    tokens,
    block_ids,
    cotangent,
    gain_first,
    w_query,
    w_key,
    w_value,
    w_output,
    gain_second,
    w_gate,
    w_up,
    w_down,
    moment_first,
    moment_query,
    moment_key,
    moment_value,
    moment_output,
    moment_second,
    moment_gate,
    moment_up,
    moment_down,
    step,
    rate,
):
    seqs, length = block_ids.shape
    count = tokens.shape[0]
    scale = 1.0 / math.sqrt(HD)
    group = H // KV
    (
        gain_one,
        query_weight,
        key_weight,
        value_weight,
        output_weight,
        gain_two,
        gate_weight,
        up_weight,
        down_weight,
    ) = (
        lax.all_gather(gain_first.astype(jnp.bfloat16), "dp", axis=0, tiled=True),
        lax.all_gather(w_query.astype(jnp.bfloat16), "dp", axis=0, tiled=True),
        lax.all_gather(w_key.astype(jnp.bfloat16), "dp", axis=0, tiled=True),
        lax.all_gather(w_value.astype(jnp.bfloat16), "dp", axis=0, tiled=True),
        lax.all_gather(w_output.astype(jnp.bfloat16), "dp", axis=1, tiled=True),
        lax.all_gather(gain_second.astype(jnp.bfloat16), "dp", axis=0, tiled=True),
        lax.all_gather(w_gate.astype(jnp.bfloat16), "dp", axis=0, tiled=True),
        lax.all_gather(w_up.astype(jnp.bfloat16), "dp", axis=0, tiled=True),
        lax.all_gather(w_down.astype(jnp.bfloat16), "dp", axis=1, tiled=True),
    )
    heads_local = query_weight.shape[1] // HD
    kv_local = key_weight.shape[1] // HD
    inputs = tokens.astype(jnp.float32)
    inverse_first = inverse_rms(inputs)
    gain_one_wide = gain_one.astype(jnp.float32)
    normed = (inputs * inverse_first * gain_one_wide[None, :]).astype(jnp.bfloat16)
    cosine, sine = angle_table(count, length)
    query = rotate(
        jnp.dot(normed, query_weight, preferred_element_type=jnp.float32).reshape(
            count, heads_local, HD
        ),
        cosine,
        sine,
    ).astype(jnp.bfloat16)
    key = rotate(
        jnp.dot(normed, key_weight, preferred_element_type=jnp.float32).reshape(
            count, kv_local, HD
        ),
        cosine,
        sine,
    ).astype(jnp.bfloat16)
    value = (
        jnp.dot(normed, value_weight, preferred_element_type=jnp.float32)
        .astype(jnp.bfloat16)
        .reshape(count, kv_local, HD)
    )
    query_items = to_items(query.reshape(count, kv_local, group, HD), seqs, length)
    key_items = to_items(key, seqs, length)
    value_items = to_items(value, seqs, length)
    block_items = jnp.repeat(block_ids, kv_local, axis=0)
    mixed_items, peak, total = lax.map(
        attend_forward(scale), (query_items, key_items, value_items, block_items)
    )
    mixed = from_items(mixed_items, seqs).reshape(count, heads_local * HD)
    hidden = inputs + lax.psum(
        jnp.dot(mixed, output_weight, preferred_element_type=jnp.float32).astype(jnp.bfloat16),
        "shard",
    ).astype(jnp.float32)
    inverse_second = inverse_rms(hidden)
    gain_two_wide = gain_two.astype(jnp.float32)
    normed_two = (hidden * inverse_second * gain_two_wide[None, :]).astype(jnp.bfloat16)
    gate = jnp.dot(normed_two, gate_weight, preferred_element_type=jnp.float32)
    up = jnp.dot(normed_two, up_weight, preferred_element_type=jnp.float32)
    sigmoid_gate = jax.nn.sigmoid(gate)
    activated = (gate * sigmoid_gate * up).astype(jnp.bfloat16)
    result = hidden + lax.psum(
        jnp.dot(activated, down_weight, preferred_element_type=jnp.float32).astype(jnp.bfloat16),
        "shard",
    ).astype(jnp.float32)
    output = result.astype(jnp.bfloat16)
    grad_result = cotangent.astype(jnp.float32)
    grad_down_weight = jnp.einsum(
        "tf,td->fd", activated, cotangent, preferred_element_type=jnp.float32
    )
    grad_act = jnp.einsum("td,fd->tf", cotangent, down_weight, preferred_element_type=jnp.float32)
    grad_gate_in = (grad_act * up * sigmoid_gate * (1.0 + gate * (1.0 - sigmoid_gate))).astype(
        jnp.bfloat16
    )
    grad_up_in = (grad_act * gate * sigmoid_gate).astype(jnp.bfloat16)
    grad_gate_weight = jnp.einsum(
        "tc,tf->cf", normed_two, grad_gate_in, preferred_element_type=jnp.float32
    )
    grad_up_weight = jnp.einsum(
        "tc,tf->cf", normed_two, grad_up_in, preferred_element_type=jnp.float32
    )
    partial_two = jnp.einsum(
        "tf,cf->tc", grad_gate_in, gate_weight, preferred_element_type=jnp.float32
    ) + jnp.einsum("tf,cf->tc", grad_up_in, up_weight, preferred_element_type=jnp.float32)
    grad_normed_two = lax.psum(partial_two.astype(jnp.bfloat16), "shard").astype(jnp.float32)
    gain_grad_two, grad_through = norm_back(hidden, inverse_second, gain_two_wide, grad_normed_two)
    grad_hidden = grad_result + grad_through
    grad_hidden_low = grad_hidden.astype(jnp.bfloat16)
    grad_output_weight = jnp.einsum(
        "tk,td->kd", mixed, grad_hidden_low, preferred_element_type=jnp.float32
    )
    grad_mixed = jnp.einsum(
        "td,kd->tk", grad_hidden_low, output_weight, preferred_element_type=jnp.float32
    ).astype(jnp.bfloat16)
    grad_mixed_items = to_items(grad_mixed.reshape(count, kv_local, group, HD), seqs, length)
    grad_query_items, grad_key_items, grad_value_items = lax.map(
        attend_backward(scale),
        (query_items, key_items, value_items, block_items, peak, total, grad_mixed_items),
    )
    grad_query_in = (
        unrotate(from_items(grad_query_items, seqs).reshape(count, heads_local, HD), cosine, sine)
        .astype(jnp.bfloat16)
        .reshape(count, heads_local * HD)
    )
    grad_key_in = (
        unrotate(from_items(grad_key_items, seqs), cosine, sine)
        .astype(jnp.bfloat16)
        .reshape(count, kv_local * HD)
    )
    grad_value_in = (
        from_items(grad_value_items, seqs).astype(jnp.bfloat16).reshape(count, kv_local * HD)
    )
    grad_query_weight = jnp.einsum(
        "tc,tk->ck", normed, grad_query_in, preferred_element_type=jnp.float32
    )
    grad_key_weight = jnp.einsum(
        "tc,tk->ck", normed, grad_key_in, preferred_element_type=jnp.float32
    )
    grad_value_weight = jnp.einsum(
        "tc,tk->ck", normed, grad_value_in, preferred_element_type=jnp.float32
    )
    partial_one = jnp.einsum(
        "tk,ck->tc", grad_query_in, query_weight, preferred_element_type=jnp.float32
    )
    partial_one = partial_one + jnp.einsum(
        "tk,ck->tc", grad_key_in, key_weight, preferred_element_type=jnp.float32
    )
    partial_one = partial_one + jnp.einsum(
        "tk,ck->tc", grad_value_in, value_weight, preferred_element_type=jnp.float32
    )
    grad_normed = lax.psum(partial_one.astype(jnp.bfloat16), "shard").astype(jnp.float32)
    gain_grad_one, grad_inner = norm_back(inputs, inverse_first, gain_one_wide, grad_normed)
    input_grad = grad_hidden + grad_inner
    owned = (
        lax.psum_scatter(
            gain_grad_one.astype(jnp.bfloat16), "dp", scatter_dimension=0, tiled=True
        ).astype(jnp.float32),
        lax.psum_scatter(
            grad_query_weight.astype(jnp.bfloat16), "dp", scatter_dimension=0, tiled=True
        ).astype(jnp.float32),
        lax.psum_scatter(
            grad_key_weight.astype(jnp.bfloat16), "dp", scatter_dimension=0, tiled=True
        ).astype(jnp.float32),
        lax.psum_scatter(
            grad_value_weight.astype(jnp.bfloat16), "dp", scatter_dimension=0, tiled=True
        ).astype(jnp.float32),
        lax.psum_scatter(
            grad_output_weight.astype(jnp.bfloat16), "dp", scatter_dimension=1, tiled=True
        ).astype(jnp.float32),
        lax.psum_scatter(
            gain_grad_two.astype(jnp.bfloat16), "dp", scatter_dimension=0, tiled=True
        ).astype(jnp.float32),
        lax.psum_scatter(
            grad_gate_weight.astype(jnp.bfloat16), "dp", scatter_dimension=0, tiled=True
        ).astype(jnp.float32),
        lax.psum_scatter(
            grad_up_weight.astype(jnp.bfloat16), "dp", scatter_dimension=0, tiled=True
        ).astype(jnp.float32),
        lax.psum_scatter(
            grad_down_weight.astype(jnp.bfloat16), "dp", scatter_dimension=1, tiled=True
        ).astype(jnp.float32),
    )
    first_shard = (lax.axis_index("shard") == 0).astype(jnp.float32)
    squares = first_shard * (jnp.sum(owned[0] * owned[0]) + jnp.sum(owned[5] * owned[5]))
    for position in (1, 2, 3, 4, 6, 7, 8):
        squares = squares + jnp.sum(owned[position] * owned[position])
    global_norm = jnp.sqrt(lax.psum(squares, ("dp", "shard")))
    factor = jnp.minimum(1.0, CLIP / global_norm)
    rate_now = rate * jnp.minimum(1.0, (step.astype(jnp.float32) + 1.0) / WARMUP)
    masters = (gain_first, w_query, w_key, w_value, w_output, gain_second, w_gate, w_up, w_down)
    moments = (
        moment_first,
        moment_query,
        moment_key,
        moment_value,
        moment_output,
        moment_second,
        moment_gate,
        moment_up,
        moment_down,
    )
    momenta = [0.5 * moment + 0.5 * (factor * gradient) for moment, gradient in zip(moments, owned)]
    updated = [master - rate_now * momentum for master, momentum in zip(masters, momenta)]
    return (
        output,
        input_grad,
        global_norm,
        momenta[0],
        momenta[1],
        momenta[2],
        momenta[3],
        momenta[4],
        momenta[5],
        momenta[6],
        momenta[7],
        momenta[8],
        updated[0],
        updated[1],
        updated[2],
        updated[3],
        updated[4],
        updated[5],
        updated[6],
        updated[7],
        updated[8],
    )


def solution(mesh):
    in_specs = (
        P("dp", None),
        P("dp", None),
        P("dp", None),
        P("dp"),
        P("dp", "shard"),
        P("dp", "shard"),
        P("dp", "shard"),
        P("shard", "dp"),
        P("dp"),
        P("dp", "shard"),
        P("dp", "shard"),
        P("shard", "dp"),
        P("dp"),
        P("dp", "shard"),
        P("dp", "shard"),
        P("dp", "shard"),
        P("shard", "dp"),
        P("dp"),
        P("dp", "shard"),
        P("dp", "shard"),
        P("shard", "dp"),
        P(),
        P(),
    )
    out_specs = (
        P("dp", None),
        P("dp", None),
        P(),
        P("dp"),
        P("dp", "shard"),
        P("dp", "shard"),
        P("dp", "shard"),
        P("shard", "dp"),
        P("dp"),
        P("dp", "shard"),
        P("dp", "shard"),
        P("shard", "dp"),
        P("dp"),
        P("dp", "shard"),
        P("dp", "shard"),
        P("dp", "shard"),
        P("shard", "dp"),
        P("dp"),
        P("dp", "shard"),
        P("dp", "shard"),
        P("shard", "dp"),
    )
    return jax.shard_map(
        on_device, mesh=mesh, in_specs=in_specs, out_specs=out_specs, check_vma=False
    )
```

profile of v0, /device:TPU:0, one launch (start us, length us, event | category | flops | bytes accessed | tf_op | source)
XLA Modules:
  0.0 1819.1 jit_solution(10321602777745166804)
XLA Ops:
  11.8 22.4 %all-gather = bf16[8,1,256]{2,1,0:T(2,128)(2,1)S(1)} all-gather(bf16[1,1,256]{2,1,0:T(2,128)(2,1)S(1)} %reshape.331), channel_id=1, replica_groups=mesh['dp'=8,'shard'=4] {'dp'}, dimensions={0}, use_global_device_ids=true | all-gather | bytes 4608 | tf_op jit(solution)/shard_map/all_gather | solution.py:157
  34.3 3.1 fusion.66
  38.9 32.9 %all_gather.28 = bf16[2048,128]{1,0:T(8,128)(2,1)S(1)} all-gather(bf16[256,128]{1,0:T(8,128)(2,1)S(1)} %convert_element_type.243), channel_id=1, replica_groups=mesh['dp'=8,'shard'=4] {'dp'}, dimensions={0}, use_global_device_ids=true | all-gather | bytes 589824 | tf_op jit(solution)/shard_map/all_gather | solution.py:160
  72.8 31.7 %all_gather.29 = bf16[2048,128]{1,0:T(8,128)(2,1)S(1)} all-gather(bf16[256,128]{1,0:T(8,128)(2,1)S(1)} %convert_element_type.245), channel_id=1, replica_groups=mesh['dp'=8,'shard'=4] {'dp'}, dimensions={0}, use_global_device_ids=true | all-gather | bytes 589824 | tf_op jit(solution)/shard_map/all_gather | solution.py:159
  110.5 5.3 fusion.111
  116.8 30.4 %while.28 = (s32[]{:T(128)}, bf16[2,1024,4,64]{1,3,2,0:T(8,128)(2,1)}, f32[2,4,1024,1]{2,1,3,0:T(4,128)}, f32[2,4,1024,1]{2,1,3,0:T(4,128)}, bf16[2,1024,64]{1,2...) while((s32[]{:T(128)}, ...), condition=%wide.region_4.5_spmd, body=%wide.region_1.4_spmd.sunk | while | flops 1125376000 | bytes 64387236 | solution.py:197
  118.5 3.9 fusion.178
  122.4 3.7 fusion.179
  126.0 5.1 fusion.180
  133.5 3.9 fusion.178
  137.4 3.7 fusion.179
  141.1 5.1 fusion.180
  147.2 6.7 convolution_convert_fusion.4
  155.2 2.7 convert_element_type.255
  158.0 2.7 convert_element_type.257
  160.8 16.6 all-gather.1
  177.3 59.9 %all-reduce.8.cloned.1.call-done = bf16[1024,2048]{1,0:T(8,128)(2,1)} async-done(((bf16[1024,2048]{1,0:T(8,128)(2,1)}), bf16[1024,2048]{1,0:T(8,128)(2,1)}) %all-reduce.8.cloned.1.call-update) | async-done | bytes 4194320 | tf_op jit(solution)/shard_map/psum | solution.py:201
  237.2 5.0 multiply_reduce_fusion
  243.2 4.6 multiply_convert_fusion.3
  247.8 117.3 %all-gather.12.cloned.1.call-done = bf16[2048,2048]{1,0:T(8,128)(2,1)} async-done(((bf16[256,2048]{1,0:T(8,128)(2,1)}), bf16[2048,2048]{1,0:T(8,128)(2,1)}) %all-gather.12.cloned.1.call-update) | async-done | bytes 8388624 | tf_op jit(solution)/shard_map/all_gather | solution.py:163
  365.1 14.5 fusion.112
  379.6 111.4 %all-gather.14.cloned.1.call-done = bf16[2048,2048]{1,0:T(8,128)(2,1)} async-done(((bf16[256,2048]{1,0:T(8,128)(2,1)}), bf16[2048,2048]{1,0:T(8,128)(2,1)}) %all-gather.14.cloned.1.call-update) | async-done | bytes 8388624 | tf_op jit(solution)/shard_map/all_gather | solution.py:164
  491.0 14.5 fusion.113
  505.5 111.8 %all-gather.16.cloned.1.call-done = bf16[2048,2048]{1,0:T(8,128)(2,1)} async-done(((bf16[2048,256]{1,0:T(8,128)(2,1)}), bf16[2048,2048]{1,0:T(8,128)(2,1)}) %all-gather.16.cloned.1.call-update) | async-done | bytes 8388624 | tf_op jit(solution)/shard_map/all_gather | solution.py:165
  617.3 22.1 %multiply_convert_fusion = (bf16[1024,2048]{1,0:T(8,128)(2,1)}, bf16[1024,2048]{1,0:T(8,128)(2,1)}, bf16[1024,2048]{1,0:T(8,128)(2,1)}) fusion(f32[1024,2048]{1,0:T(8,128)} %fusion.112, f32[1024,2048]{1,0:T(8,128)} %fusion.113, bf16[1024,2048]{1,0:T(8,128)(2,1)} %param.29, bf16[2048,2048]{1,0:T(8,128)(2,1)} %all-gather.16.cloned.1.call-done), kind=kOutput, calls=%fused_computation.96 | convolution fusion | flops 8623489024 | bytes 41943040 | tf_op jit(solution)/shard_map/td,fd->tf/dot_general | solution.py:221
  639.4 14.7 fusion.114
  654.1 12.2 add_convert_fusion.1
  666.4 83.8 %all-reduce.10.cloned.1.call-done = bf16[1024,2048]{1,0:T(8,128)(2,1)} async-done(((bf16[1024,2048]{1,0:T(8,128)(2,1)}), bf16[1024,2048]{1,0:T(8,128)(2,1)}) %all-reduce.10.cloned.1.call-update) | async-done | bytes 4194320 | tf_op jit(solution)/shard_map/psum | solution.py:235
  750.1 8.8 fusion.65
  758.9 5.2 fusion.62
  767.5 79.0 %while.29 = (s32[]{:T(128)}, f32[2,1024,4,64]{1,3,2,0:T(8,128)}, f32[2,1024,64]{1,2,0:T(8,128)}, bf16[2,1024,64]{1,2,0:T(8,128)(2,1)}, bf16[2,1024,64]{1,2,0:T(8...) while((s32[]{:T(128)}, f32[2,1024,4,64]{1,3,2,0:T(8,128)}, ...), condition=%wide.region_12.13_spmd, body=%wide.region_10.12_spmd.sunk | while | flops 2727669760 | bytes 159401328 | solution.py:246
  767.5 8.1 fusion.189
  778.4 11.7 fusion.190
  790.1 8.0 fusion.191
  798.2 2.6 fusion.192
  800.9 2.7 fusion.193
  803.6 2.7 fusion.194
  807.0 8.1 fusion.189
  817.8 11.7 fusion.190
  829.5 8.0 fusion.191
  840.3 2.7 fusion.193
  843.0 2.7 fusion.194
  847.7 4.3 convolution_convert_fusion.8
  852.1 13.9 convolution_convert_fusion.3
  868.7 4.0 fusion.115
  874.0 3.3 add_convert_fusion
  877.6 6.0 convolution_convert_fusion.6
  883.6 7.0 convolution_convert_fusion.5
  890.8 14.0 convolution_convert_fusion.2
  905.3 14.1 convolution_convert_fusion.1
  919.4 14.1 convolution_convert_fusion
  937.6 41.8 %reduce-scatter.12.cloned.1.call-done = bf16[256,128]{1,0:T(8,128)(2,1)} async-done(((bf16[2048,128]{1,0:T(8,128)(2,1)}), bf16[256,128]{1,0:T(8,128)(2,1)}) %reduce-scatter.12.cloned.1.call-update) | async-done | bytes 65552 | tf_op jit(solution)/shard_map/reduce_scatter | solution.py:294
  980.9 153.2 %all-reduce.12.cloned.1.call-done = (bf16[1024,2048]{1,0:T(8,128)(2,1)}, bf16[1024,2048]{1,0:T(8,128)(2,1)}) async-done(((bf16[1024,2048]{1,0:T(8,128)(2,1)}, bf16[1024,2048]{1,0:T(8,128)(2,1)}), (bf16[1024,2048]{1,0:T(8,128)(2,1)}, bf16[1024,2048]{1,0:T(8,128)(2,1)})) %all-reduce.12.cloned.1.call-update) | async-done | bytes 8388624 | tf_op jit(solution)/shard_map/psum | solution.py:212
  1134.1 5.6 fusion.72
  1139.8 22.3 %all-reduce.2 = (bf16[2048]{0:T(1024)(128)(2,1)S(1)}, bf16[2048]{0:T(1024)(128)(2,1)S(1)}) all-reduce(bf16[2048]{0:T(1024)(128)(2,1)S(1)} %get-tuple-element.132, bf16[2048]{0:T(1024)(128)(2,1)S(1)} %copy-done.43), channel_id=2, replica_groups=mesh['dp'=8,'shard'=4] {'dp'}, use_global_device_ids=true, to_apply=%region_16.17.clone | all-reduce | flops 4096 | bytes 16384
  1164.1 41.8 %reduce-scatter.8.cloned.1.call-done = bf16[256,512]{1,0:T(8,128)(2,1)} async-done(((bf16[2048,512]{1,0:T(8,128)(2,1)}), bf16[256,512]{1,0:T(8,128)(2,1)}) %reduce-scatter.8.cloned.1.call-update) | async-done | bytes 262160 | tf_op jit(solution)/shard_map/reduce_scatter | solution.py:288
  1209.5 67.7 %reduce-scatter.14.cloned.1.call-done = bf16[512,256]{1,0:T(8,128)(2,1)} async-done(((bf16[512,2048]{1,0:T(8,128)(2,1)}), bf16[512,256]{1,0:T(8,128)(2,1)}) %reduce-scatter.14.cloned.1.call-update) | async-done | bytes 262160 | tf_op jit(solution)/shard_map/reduce_scatter | solution.py:297
  1280.1 148.8 %reduce-scatter.16.cloned.1.call-done = bf16[256,2048]{1,0:T(8,128)(2,1)} async-done(((bf16[2048,2048]{1,0:T(8,128)(2,1)}), bf16[256,2048]{1,0:T(8,128)(2,1)}) %reduce-scatter.16.cloned.1.call-update) | async-done | bytes 1048592 | tf_op jit(solution)/shard_map/reduce_scatter | solution.py:303
  1431.9 148.9 %reduce-scatter.18.cloned.1.call-done = bf16[256,2048]{1,0:T(8,128)(2,1)} async-done(((bf16[2048,2048]{1,0:T(8,128)(2,1)}), bf16[256,2048]{1,0:T(8,128)(2,1)}) %reduce-scatter.18.cloned.1.call-update) | async-done | bytes 1048592 | tf_op jit(solution)/shard_map/reduce_scatter | solution.py:306
  1583.9 148.9 %reduce-scatter.20.cloned.1.call-done = bf16[2048,256]{1,0:T(8,128)(2,1)} async-done(((bf16[2048,2048]{1,0:T(8,128)(2,1)}), bf16[2048,256]{1,0:T(8,128)(2,1)}) %reduce-scatter.20.cloned.1.call-update) | async-done | bytes 1048592 | tf_op jit(solution)/shard_map/reduce_scatter | solution.py:309
  1735.9 14.7 fusion.60
  1750.7 39.0 %psum.39 = f32[]{:T(128)} all-reduce(f32[]{:T(128)S(6)} %add.221), channel_id=1, replica_groups=mesh['dp'=8,'shard'=4] {'dp','shard'}, use_global_device_ids=true, to_apply=%region_35.36 | all-reduce | flops 1 | bytes 8 | tf_op jit(solution)/shard_map/psum | solution.py:317
  1801.5 4.4 multiply_subtract_fusion.2
  1805.9 2.9 multiply_subtract_fusion.1
  (229 shorter events, 68.7 us)
Async XLA Ops:
  7.2 103.3 %all-gather.8.cloned.1.call-start = ((), (), s32[]{:S(2)}) async-start(), calls=%async_computation.7 | async-start | bytes 2359296 | tf_op jit(solution)/shard_map/all_gather | solution.py:158
  9.0 138.2 %all-gather.10.cloned.1.call-start = ((), (), s32[]{:S(2)}) async-start(), calls=%async_computation.8 | async-start | bytes 2359296 | tf_op jit(solution)/shard_map/all_gather | solution.py:161
  10.9 226.4 %all-reduce.8.cloned.1.call-start = ((), (), s32[]{:S(2)}) async-start(), calls=%async_computation.9 | async-start | bytes 8388608 | tf_op jit(solution)/shard_map/psum | solution.py:201
  11.0 93.5 %copy-start = (bf16[1024,2048]{1,0:T(8,128)(2,1)S(1)}, bf16[1024,2048]{1,0:T(8,128)(2,1)}, u32[]{:S(2)}) copy-start(bf16[1024,2048]{1,0:T(8,128)(2,1)} %param.27) | copy-start | bytes 12582916
  34.3 72.8 %copy-start.38 = (f32[8,1,256]{2,1,0:T(1,128)}, f32[8,1,256]{2,1,0:T(1,128)S(1)}, u32[]{:S(2)}) copy-start(f32[8,1,256]{2,1,0:T(1,128)S(1)} %convert_element_type.295) | copy-start | bytes 24580
  38.0 71.1 %copy-start.40 = (f32[1024]{0:T(1024)}, f32[1024]{0:T(1024)S(1)}, u32[]{:S(2)}) copy-start(f32[1024]{0:T(1024)S(1)} %get-tuple-element.218) | copy-start | bytes 12292
  71.7 37.3 %copy-start.15 = (bf16[2048,128]{1,0:T(8,128)(2,1)}, bf16[2048,128]{1,0:T(8,128)(2,1)S(1)}, u32[]{:S(2)}) copy-start(bf16[2048,128]{1,0:T(8,128)(2,1)S(1)} %all_gather.28) | copy-start | bytes 1572868
  104.5 4.6 copy-start.17
  109.7 6.1 copy-start.22
  109.7 6.1 copy-start.24
  110.5 5.7 copy-start.44
  122.3 3.7 copy-start.50
  147.2 7.9 copy-start.9
  147.2 6.8 copy-start.11
  153.9 6.8 copy-start.45
  154.0 211.2 %all-gather.12.cloned.1.call-start = ((), (), s32[]{:S(2)}) async-start(), calls=%async_computation.10 | async-start | bytes 9437184 | tf_op jit(solution)/shard_map/all_gather | solution.py:163
  155.2 335.8 %all-gather.14.cloned.1.call-start = ((), (), s32[]{:S(2)}) async-start(), calls=%async_computation.11 | async-start | bytes 9437184 | tf_op jit(solution)/shard_map/all_gather | solution.py:164
  157.9 459.3 %all-gather.16.cloned.1.call-start = ((), (), s32[]{:S(2)}) async-start(), calls=%async_computation.12 | async-start | bytes 9437184 | tf_op jit(solution)/shard_map/all_gather | solution.py:165
  160.7 589.4 %all-reduce.10.cloned.1.call-start = ((), (), s32[]{:S(2)}) async-start(), calls=%async_computation.13 | async-start | bytes 8388608 | tf_op jit(solution)/shard_map/psum | solution.py:235
  237.2 5.0 copy-start.1
  237.2 5.9 copy-start.3
  639.4 14.7 copy-start.48
  639.4 14.7 copy-start.54
  666.3 269.8 %reduce-scatter.10.cloned.1.call-start = ((), (), s32[]{:S(2)}) async-start(), calls=%async_computation.15 | async-start | bytes 589824 | tf_op jit(solution)/shard_map/reduce_scatter | solution.py:291
  750.1 8.8 copy-start.2
  750.1 8.8 copy-start.4
  750.1 8.8 copy-start.8
  758.9 5.2 copy-start.49
  767.5 79.0 %copy-start.23 = (f32[1024,32]{0,1:T(8,128)S(1)}, f32[1024,32]{0,1:T(8,128)}, u32[]{:S(2)}) copy-start(f32[1024,32]{0,1:T(8,128)} %copy-done.22) | copy-start | bytes 393220
  767.5 79.0 %copy-start.25 = (f32[1024,32]{0,1:T(8,128)S(1)}, f32[1024,32]{0,1:T(8,128)}, u32[]{:S(2)}) copy-start(f32[1024,32]{0,1:T(8,128)} %copy-done.24) | copy-start | bytes 393220
  790.1 8.1 copy-start.28
  798.2 5.3 copy-start.35
  800.8 5.4 copy-start.29
  829.5 8.1 copy-start.28
  837.6 5.3 copy-start.35
  840.2 5.4 copy-start.29
  852.0 127.5 %reduce-scatter.12.cloned.1.call-start = ((), (), s32[]{:S(2)}) async-start(), calls=%async_computation.16 | async-start | bytes 589824 | tf_op jit(solution)/shard_map/reduce_scatter | solution.py:294
  852.0 14.0 copy-start.30
  852.0 14.4 copy-start.6
  852.1 14.4 copy-start.37
  866.5 6.2 copy-start.18
  868.6 265.5 %all-reduce.12.cloned.1.call-start = ((), (), s32[]{:S(2)}) async-start(), calls=%async_computation.21 | async-start | bytes 16777216 | tf_op jit(solution)/shard_map/psum | solution.py:212
  877.3 6.3 copy-start.52
  877.3 328.6 %reduce-scatter.8.cloned.1.call-start = ((), (), s32[]{:S(2)}) async-start(), calls=%async_computation.14 | async-start | bytes 2359296 | tf_op jit(solution)/shard_map/reduce_scatter | solution.py:288
  883.6 393.6 %reduce-scatter.14.cloned.1.call-start = ((), (), s32[]{:S(2)}) async-start(), calls=%async_computation.17 | async-start | bytes 2359296 | tf_op jit(solution)/shard_map/reduce_scatter | solution.py:297
  890.7 538.2 %reduce-scatter.16.cloned.1.call-start = ((), (), s32[]{:S(2)}) async-start(), calls=%async_computation.18 | async-start | bytes 9437184 | tf_op jit(solution)/shard_map/reduce_scatter | solution.py:303
  904.8 676.1 %reduce-scatter.18.cloned.1.call-start = ((), (), s32[]{:S(2)}) async-start(), calls=%async_computation.19 | async-start | bytes 9437184 | tf_op jit(solution)/shard_map/reduce_scatter | solution.py:306
  919.4 813.5 %reduce-scatter.20.cloned.1.call-start = ((), (), s32[]{:S(2)}) async-start(), calls=%async_computation.20 | async-start | bytes 9437184 | tf_op jit(solution)/shard_map/reduce_scatter | solution.py:309
  933.5 200.6 %copy-start.39 = (f32[8,1,256]{2,1,0:T(1,128)S(1)}, f32[8,1,256]{2,1,0:T(1,128)}, u32[]{:S(2)}) copy-start(f32[8,1,256]{2,1,0:T(1,128)} %copy-done.38) | copy-start | bytes 24580
  933.5 200.6 %copy-start.41 = (f32[1024]{0:T(1024)S(1)}, f32[1024]{0:T(1024)}, u32[]{:S(2)}) copy-start(f32[1024]{0:T(1024)} %copy-done.40) | copy-start | bytes 12292
  933.5 206.3 %copy-start.43 = (bf16[2048]{0:T(1024)(128)(2,1)S(1)}, bf16[2048]{0:T(1024)(128)(2,1)}, u32[]{:S(2)}) copy-start(bf16[2048]{0:T(1024)(128)(2,1)} %get-tuple-element.130) | copy-start | bytes 12292
  933.5 802.4 %copy-start.42 = (f32[1024]{0:T(1024)S(1)}, f32[1024]{0:T(1024)}, u32[]{:S(2)}) copy-start(f32[1024]{0:T(1024)} %get-tuple-element.217) | copy-start | bytes 12292
  1162.1 573.8 %copy-start.46 = (bf16[2048]{0:T(1024)(128)(2,1)}, bf16[2048]{0:T(1024)(128)(2,1)S(1)}, u32[]{:S(2)}) copy-start(bf16[2048]{0:T(1024)(128)(2,1)S(1)} %get-tuple-element.173) | copy-start | bytes 12292
  1162.1 573.8 %copy-start.47 = (bf16[2048]{0:T(1024)(128)(2,1)}, bf16[2048]{0:T(1024)(128)(2,1)S(1)}, u32[]{:S(2)}) copy-start(bf16[2048]{0:T(1024)(128)(2,1)S(1)} %get-tuple-element.172) | copy-start | bytes 12292
  1735.9 57.5 %copy-start.31 = (bf16[256,512]{1,0:T(8,128)(2,1)S(1)}, bf16[256,512]{1,0:T(8,128)(2,1)}, u32[]{:S(2)}) copy-start(bf16[256,512]{1,0:T(8,128)(2,1)} %reduce-scatter.8.cloned.1.call-done) | copy-start | bytes 786436
  1735.9 59.9 %copy-start.34 = (f32[256,128]{1,0:T(8,128)S(1)}, f32[256,128]{1,0:T(8,128)}, u32[]{:S(2)}) copy-start(f32[256,128]{1,0:T(8,128)} %param.32) | copy-start | bytes 393220
  1735.9 65.5 %copy-start.12 = (f32[256,2048]{1,0:T(8,128)S(1)}, f32[256,2048]{1,0:T(8,128)}, u32[]{:S(2)}) copy-start(f32[256,2048]{1,0:T(8,128)} %param.36) | copy-start | bytes 6291460
  1735.9 65.5 %copy-start.19 = (bf16[256,2048]{1,0:T(8,128)(2,1)S(1)}, bf16[256,2048]{1,0:T(8,128)(2,1)}, u32[]{:S(2)}) copy-start(bf16[256,2048]{1,0:T(8,128)(2,1)} %reduce-scatter.16.cloned.1.call-done) | copy-start | bytes 3145732
  1790.5 15.5 copy-start.13
  1790.5 15.5 copy-start.20
  1790.5 15.4 copy-start.26
  1801.4 7.4 copy-start.14
  1801.5 7.4 copy-start.21
  1801.5 7.3 copy-start.27
  (15 other events, 31.2 us)
Sparse Core Ops, SparseCore 0:
  10.7 58.7 all-gather.7
  72.2 52.4 all-gather.9
  154.1 83.1 all-reduce.7
  240.0 125.0 all-gather.11
  367.9 123.0 all-gather.13
  493.7 123.5 all-gather.15
  666.4 83.6 all-reduce.9
  852.1 62.0 reduce-scatter.9
  918.5 60.9 reduce-scatter.11
  981.9 152.2 all-reduce.11
  1138.2 67.5 reduce-scatter.7
  1209.8 67.3 reduce-scatter.13
  1280.8 148.0 reduce-scatter.15
  1432.8 148.0 reduce-scatter.17
  1584.4 148.4 reduce-scatter.19
where the time goes:
time: 1830 us; the launch traced here: 1820 us
  waiting for transfers between devices  1240 us (68%)
  matrix products  253 us (14%)
  blocking collectives  165 us (9%)
  other arithmetic  126 us (7%)
  between operations  24.5 us (1%)
    psum x1, waiting for transfers between devices, on_device(): lax.psum(jnp.dot(activated, down_weight, preferred_element_type=jnp.float...  153 us
    reduce_scatter x1, waiting for transfers between devices, on_device(): lax.psum_scatter(grad_up_weight.astype(jnp.bfloat16), 'dp', scatter_dimen...  149 us
    reduce_scatter x1, waiting for transfers between devices, on_device(): lax.psum_scatter(grad_down_weight.astype(jnp.bfloat16), 'dp', scatter_dim...  149 us
    reduce_scatter x1, waiting for transfers between devices, on_device(): lax.psum_scatter(grad_gate_weight.astype(jnp.bfloat16), 'dp', scatter_dim...  149 us
    all_gather x1, waiting for transfers between devices, on_device(): lax.all_gather(w_gate.astype(jnp.bfloat16), 'dp', axis=0, tiled=True)  117 us
    all_gather x1, waiting for transfers between devices, on_device(): lax.all_gather(w_down.astype(jnp.bfloat16), 'dp', axis=1, tiled=True)  112 us
    all_gather x1, waiting for transfers between devices, on_device(): lax.all_gather(w_up.astype(jnp.bfloat16), 'dp', axis=0, tiled=True)  111 us
    psum x1, waiting for transfers between devices, on_device(): lax.psum(partial_two.astype(jnp.bfloat16), 'shard').astype(jnp.float32)  83.8 us
  transfers between devices with their start and end apart: 15, of which 12 were waited for; matrix products, arithmetic and copies ran while one was open for 11% of the time, Pallas kernels for 0%

commit v1 on v0

--- a/solution.py
+++ b/solution.py
@@ -12,6 +12,27 @@
 EPS = 1e-05
 THETA = 10000000.0
 NEGATIVE = -1e30
+
+
+def gather_around(value, axis, dim):
+    size, index, width = (lax.axis_size(axis), lax.axis_index(axis), value.shape[dim])
+    right = [(i, (i + 1) % size) for i in range(size)]
+    left = [(i, (i - 1) % size) for i in range(size)]
+    out = jnp.zeros((*value.shape[:dim], size * width, *value.shape[dim + 1 :]), value.dtype)
+    out = lax.dynamic_update_slice_in_dim(out, value, index * width, axis=dim)
+    from_left = from_right = value
+    middle = size // 2
+    for hop in range(1, middle + 1):
+        from_left = lax.ppermute(from_left, axis, right)
+        out = lax.dynamic_update_slice_in_dim(
+            out, from_left, (index - hop) % size * width, axis=dim
+        )
+        if hop < size - middle:
+            from_right = lax.ppermute(from_right, axis, left)
+            out = lax.dynamic_update_slice_in_dim(
+                out, from_right, (index + hop) % size * width, axis=dim
+            )
+    return out
 
 
 def inverse_rms(values):
@@ -161,7 +182,7 @@
         lax.all_gather(w_output.astype(jnp.bfloat16), "dp", axis=1, tiled=True),
         lax.all_gather(gain_second.astype(jnp.bfloat16), "dp", axis=0, tiled=True),
         lax.all_gather(w_gate.astype(jnp.bfloat16), "dp", axis=0, tiled=True),
-        lax.all_gather(w_up.astype(jnp.bfloat16), "dp", axis=0, tiled=True),
+        gather_around(w_up.astype(jnp.bfloat16), "dp", 0),
         lax.all_gather(w_down.astype(jnp.bfloat16), "dp", axis=1, tiled=True),
     )
     heads_local = query_weight.shape[1] // HD

time: 1830 us -> 1740 us (0.951)
  waiting for transfers between devices: 1240 us -> 1100 us
  blocking collectives: 165 us -> 200 us
    all_gather x1 -> x0, waiting for transfers between devices: 111 us -> none  [on_device(): lax.all_gather(w_up.astype(jnp.bfloat16), 'dp', axis=0, tiled=True)]
    ppermute x0 -> x7, waiting for transfers between devices: none -> 84 us  [the longest x4 72.5 us: gather_around(): from_left = lax.ppermute(from_left, axis, right)]
    psum x1, waiting for transfers between devices: 59.9 us -> 0.01 us  [on_device(): lax.psum(jnp.dot(mixed, output_weight, preferred_element_type=jnp.float32...]
    all_gather x1, waiting for transfers between devices: 112 us -> 67.9 us  [on_device(): lax.all_gather(w_down.astype(jnp.bfloat16), 'dp', axis=1, tiled=True)]
    all_gather x1, blocking collectives: 16.6 us -> 50.8 us  [on_device(): lax.all_gather(gain_second.astype(jnp.bfloat16), 'dp', axis=0, tiled=True)]
  transfers between devices with their start and end apart: 15 -> 21, of which waited for: 12 -> 14; matrix products, arithmetic and copies ran while one was open for 11% -> 11% of each run, Pallas kernels for 0% -> 0%
where the time goes in v1:
time: 1740 us; the launch traced here: 1730 us
  waiting for transfers between devices  1100 us (63%)
  matrix products  246 us (14%)
  blocking collectives  200 us (11%)
  other arithmetic  122 us (7%)
  local copies, waits for them, and re-layouts  24.8 us (1%)
  between operations  24.7 us (1%)
    psum x1, waiting for transfers between devices, on_device(): lax.psum(jnp.dot(activated, down_weight, preferred_element_type=jnp.float...  153 us
    reduce_scatter x1, waiting for transfers between devices, on_device(): lax.psum_scatter(grad_up_weight.astype(jnp.bfloat16), 'dp', scatter_dimen...  149 us
    reduce_scatter x1, waiting for transfers between devices, on_device(): lax.psum_scatter(grad_down_weight.astype(jnp.bfloat16), 'dp', scatter_dim...  149 us
    reduce_scatter x1, waiting for transfers between devices, on_device(): lax.psum_scatter(grad_gate_weight.astype(jnp.bfloat16), 'dp', scatter_dim...  149 us
    all_gather x1, waiting for transfers between devices, on_device(): lax.all_gather(w_gate.astype(jnp.bfloat16), 'dp', axis=0, tiled=True)  111 us
    psum x1, waiting for transfers between devices, on_device(): lax.psum(partial_two.astype(jnp.bfloat16), 'shard').astype(jnp.float32)  83.7 us
    ppermute x4, waiting for transfers between devices, gather_around(): from_left = lax.ppermute(from_left, axis, right)  72.5 us
    reduce_scatter x1, waiting for transfers between devices, on_device(): lax.psum_scatter(grad_output_weight.astype(jnp.bfloat16), 'dp', scatter_d...  67.9 us
  transfers between devices with their start and end apart: 21, of which 14 were waited for; matrix products, arithmetic and copies ran while one was open for 11% of the time, Pallas kernels for 0%

profile of v1, /device:TPU:0, one launch (start us, length us, event | category | flops | bytes accessed | tf_op | source)
XLA Modules:
  0.0 1732.8 jit_solution(9480047262276136352)
XLA Ops:
  11.8 22.4 %all-gather = bf16[8,1,256]{2,1,0:T(2,128)(2,1)S(1)} all-gather(bf16[1,1,256]{2,1,0:T(2,128)(2,1)S(1)} %reshape.331), channel_id=1, replica_groups=mesh['dp'=8,'shard'=4] {'dp'}, dimensions={0}, use_global_device_ids=true | all-gather | bytes 4608 | tf_op jit(solution)/shard_map/all_gather | solution.py:178
  34.3 3.1 fusion.66
  38.9 32.9 %all_gather.25 = bf16[2048,128]{1,0:T(8,128)(2,1)S(1)} all-gather(bf16[256,128]{1,0:T(8,128)(2,1)S(1)} %convert_element_type.243), channel_id=1, replica_groups=mesh['dp'=8,'shard'=4] {'dp'}, dimensions={0}, use_global_device_ids=true | all-gather | bytes 589824 | tf_op jit(solution)/shard_map/all_gather | solution.py:181
  72.8 32.0 %all_gather.26 = bf16[2048,128]{1,0:T(8,128)(2,1)S(1)} all-gather(bf16[256,128]{1,0:T(8,128)(2,1)S(1)} %convert_element_type.245), channel_id=1, replica_groups=mesh['dp'=8,'shard'=4] {'dp'}, dimensions={0}, use_global_device_ids=true | all-gather | bytes 589824 | tf_op jit(solution)/shard_map/all_gather | solution.py:180
  110.1 5.3 fusion.111
  115.9 27.1 %while.28 = (s32[]{:T(128)}, bf16[2,1024,4,64]{1,3,2,0:T(8,128)(2,1)}, f32[2,4,1024,1]{2,1,3,0:T(4,128)}, f32[2,4,1024,1]{2,1,3,0:T(4,128)}, bf16[2,1024,64]{1,2...) while((s32[]{:T(128)}, ...), condition=%wide.region_4.5_spmd, body=%wide.region_1.4_spmd.sunk | while | flops 1125376000 | bytes 64387236 | solution.py:218
  116.7 3.0 fusion.178
  119.7 3.7 fusion.179
  123.4 5.1 fusion.180
  130.2 3.0 fusion.178
  133.2 3.7 fusion.179
  136.9 5.1 fusion.180
  143.7 6.5 convolution_convert_fusion.4
  150.2 2.7 convert_element_type.257
  155.9 3.3 copy-done.16
  159.2 4.7 collective-permute-start.1
  163.9 38.5 %collective-permute-done = bf16[256,2048]{1,0:T(8,128)(2,1)S(1)} collective-permute-done((bf16[256,2048]{1,0:T(8,128)(2,1)S(1)}, bf16[256,2048]{1,0:T(8,128)(2,1)S(1)}, u32[]{:S(2)}, u32[]{:S(2)}) %collective-permute-start) | collective-permute-done | bytes 1048608 | tf_op jit(solution)/shard_map/ppermute | solution.py:26
  207.4 29.3 %collective-permute-done.2 = bf16[256,2048]{1,0:T(8,128)(2,1)} collective-permute-done((bf16[256,2048]{1,0:T(8,128)(2,1)S(1)}, bf16[256,2048]{1,0:T(8,128)(2,1)}, u32[]{:S(2)}, u32[]{:S(2)}) %collective-permute-start.2) | collective-permute-done | bytes 1048608 | tf_op jit(solution)/shard_map/ppermute | solution.py:26
  239.2 50.8 %all-gather.1 = bf16[8,1,256]{2,1,0:T(2,128)(2,1)S(1)} all-gather(bf16[1,1,256]{2,1,0:T(2,128)(2,1)S(1)} %reshape.333), channel_id=1, replica_groups=mesh['dp'=8,'shard'=4] {'dp'}, dimensions={0}, use_global_device_ids=true | all-gather | bytes 4608 | tf_op jit(solution)/shard_map/all_gather | solution.py:183
  299.9 11.6 collective-permute-done.5
  312.6 4.7 collective-permute-done.6
  318.4 5.0 multiply_reduce_fusion
  324.4 4.3 multiply_convert_fusion.3
  328.7 67.9 %all-gather.13.cloned.1.call-done = bf16[2048,2048]{1,0:T(8,128)(2,1)} async-done(((bf16[2048,256]{1,0:T(8,128)(2,1)}), bf16[2048,2048]{1,0:T(8,128)(2,1)}) %all-gather.13.cloned.1.call-update) | async-done | bytes 8388624 | tf_op jit(solution)/shard_map/all_gather | solution.py:186
  396.6 14.5 fusion.113
  411.1 111.4 %all-gather.11.cloned.1.call-done = bf16[2048,2048]{1,0:T(8,128)(2,1)} async-done(((bf16[256,2048]{1,0:T(8,128)(2,1)}), bf16[2048,2048]{1,0:T(8,128)(2,1)}) %all-gather.11.cloned.1.call-update) | async-done | bytes 8388624 | tf_op jit(solution)/shard_map/all_gather | solution.py:184
  522.5 15.6 fusion.112
  538.1 19.1 %multiply_convert_fusion = (bf16[1024,2048]{1,0:T(8,128)(2,1)}, bf16[1024,2048]{1,0:T(8,128)(2,1)}, bf16[1024,2048]{1,0:T(8,128)(2,1)}) fusion(f32[1024,2048]{1,0:T(8,128)} %fusion.113, f32[1024,2048]{1,0:T(8,128)} %fusion.112, bf16[1024,2048]{1,0:T(8,128)(2,1)S(1)} %copy-done.21, bf16[2048,2048]{1,0:T(8,128)(2,1)} %constant_dynamic-update-slice_fusion), kind=kOutput, calls=%fused_computation.96 | convolution fusion | flops 8623489024 | bytes 41943040 | tf_op jit(solution)/shard_map/dot_general | solution.py:230
  557.2 13.2 fusion.114
  570.4 12.8 add_convert_fusion.1
  583.3 83.7 %all-reduce.10.cloned.1.call-done = bf16[1024,2048]{1,0:T(8,128)(2,1)} async-done(((bf16[1024,2048]{1,0:T(8,128)(2,1)}), bf16[1024,2048]{1,0:T(8,128)(2,1)}) %all-reduce.10.cloned.1.call-update) | async-done | bytes 4194320 | tf_op jit(solution)/shard_map/psum | solution.py:256
  667.0 8.5 fusion.65
  675.6 5.2 fusion.62
  684.2 75.8 %while.29 = (s32[]{:T(128)}, f32[2,1024,4,64]{1,3,2,0:T(8,128)}, f32[2,1024,64]{1,2,0:T(8,128)}, bf16[2,1024,64]{1,2,0:T(8,128)(2,1)}, bf16[2,1024,64]{1,2,0:T(8...) while((s32[]{:T(128)}, f32[2,1024,4,64]{1,3,2,0:T(8,128)}, ...), condition=%wide.region_12.13_spmd, body=%wide.region_10.12_spmd.sunk | while | flops 2727669760 | bytes 160449936 | solution.py:267
  684.4 8.2 fusion.189
  694.5 11.7 fusion.190
  706.3 8.0 fusion.191
  716.0 2.7 fusion.193
  722.1 8.1 fusion.189
  732.3 11.7 fusion.190
  744.0 8.0 fusion.191
  753.7 2.7 fusion.193
  761.2 4.3 convolution_convert_fusion.8
  765.6 14.0 convolution_convert_fusion.3
  782.2 4.0 fusion.115
  787.5 3.3 add_convert_fusion
  791.3 5.9 convolution_convert_fusion.6
  797.3 7.0 convolution_convert_fusion.5
  804.4 14.1 convolution_convert_fusion.2
  818.8 14.1 convolution_convert_fusion.1
  832.9 14.1 convolution_convert_fusion
  851.1 41.8 %reduce-scatter.12.cloned.1.call-done = bf16[256,128]{1,0:T(8,128)(2,1)} async-done(((bf16[2048,128]{1,0:T(8,128)(2,1)}), bf16[256,128]{1,0:T(8,128)(2,1)}) %reduce-scatter.12.cloned.1.call-update) | async-done | bytes 65552 | tf_op jit(solution)/shard_map/reduce_scatter | solution.py:315
  894.4 153.4 %all-reduce.12.cloned.1.call-done = (bf16[1024,2048]{1,0:T(8,128)(2,1)}, bf16[1024,2048]{1,0:T(8,128)(2,1)}) async-done(((bf16[1024,2048]{1,0:T(8,128)(2,1)}, bf16[1024,2048]{1,0:T(8,128)(2,1)}), (bf16[1024,2048]{1,0:T(8,128)(2,1)}, bf16[1024,2048]{1,0:T(8,128)(2,1)})) %all-reduce.12.cloned.1.call-update) | async-done | bytes 8388624 | tf_op jit(solution)/shard_map/psum | solution.py:233
  1047.8 5.6 fusion.72
  1053.5 22.3 %all-reduce.2 = (bf16[2048]{0:T(1024)(128)(2,1)S(1)}, bf16[2048]{0:T(1024)(128)(2,1)S(1)}) all-reduce(bf16[2048]{0:T(1024)(128)(2,1)S(1)} %get-tuple-element.132, bf16[2048]{0:T(1024)(128)(2,1)S(1)} %copy-done.51), channel_id=2, replica_groups=mesh['dp'=8,'shard'=4] {'dp'}, use_global_device_ids=true, to_apply=%region_16.17.clone | all-reduce | flops 4096 | bytes 16384
  1077.8 41.7 %reduce-scatter.8.cloned.1.call-done = bf16[256,512]{1,0:T(8,128)(2,1)} async-done(((bf16[2048,512]{1,0:T(8,128)(2,1)}), bf16[256,512]{1,0:T(8,128)(2,1)}) %reduce-scatter.8.cloned.1.call-update) | async-done | bytes 262160 | tf_op jit(solution)/shard_map/reduce_scatter | solution.py:309
  1123.1 67.9 %reduce-scatter.14.cloned.1.call-done = bf16[512,256]{1,0:T(8,128)(2,1)} async-done(((bf16[512,2048]{1,0:T(8,128)(2,1)}), bf16[512,256]{1,0:T(8,128)(2,1)}) %reduce-scatter.14.cloned.1.call-update) | async-done | bytes 262160 | tf_op jit(solution)/shard_map/reduce_scatter | solution.py:318
  1194.0 148.6 %reduce-scatter.16.cloned.1.call-done = bf16[256,2048]{1,0:T(8,128)(2,1)} async-done(((bf16[2048,2048]{1,0:T(8,128)(2,1)}), bf16[256,2048]{1,0:T(8,128)(2,1)}) %reduce-scatter.16.cloned.1.call-update) | async-done | bytes 1048592 | tf_op jit(solution)/shard_map/reduce_scatter | solution.py:324
  1345.5 149.1 %reduce-scatter.18.cloned.1.call-done = bf16[256,2048]{1,0:T(8,128)(2,1)} async-done(((bf16[2048,2048]{1,0:T(8,128)(2,1)}), bf16[256,2048]{1,0:T(8,128)(2,1)}) %reduce-scatter.18.cloned.1.call-update) | async-done | bytes 1048592 | tf_op jit(solution)/shard_map/reduce_scatter | solution.py:327
  1497.7 148.9 %reduce-scatter.20.cloned.1.call-done = bf16[2048,256]{1,0:T(8,128)(2,1)} async-done(((bf16[2048,2048]{1,0:T(8,128)(2,1)}), bf16[2048,256]{1,0:T(8,128)(2,1)}) %reduce-scatter.20.cloned.1.call-update) | async-done | bytes 1048592 | tf_op jit(solution)/shard_map/reduce_scatter | solution.py:330
  1649.6 14.7 fusion.60
  1664.4 39.0 %psum.39 = f32[]{:T(128)} all-reduce(f32[]{:T(128)S(6)} %add.298), channel_id=1, replica_groups=mesh['dp'=8,'shard'=4] {'dp','shard'}, use_global_device_ids=true, to_apply=%region_35.36 | all-reduce | flops 1 | bytes 8 | tf_op jit(solution)/shard_map/psum | solution.py:338
  1715.2 4.4 multiply_subtract_fusion.2
  1719.6 2.9 multiply_subtract_fusion.1
  (264 shorter events, 92.5 us)
Async XLA Ops:
  7.2 102.9 %all-gather.7.cloned.1.call-start = ((), (), s32[]{:S(2)}) async-start(), calls=%async_computation.7 | async-start | bytes 2359296 | tf_op jit(solution)/shard_map/all_gather | solution.py:179
  9.0 134.0 %all-gather.9.cloned.1.call-start = ((), (), s32[]{:S(2)}) async-start(), calls=%async_computation.8 | async-start | bytes 2359296 | tf_op jit(solution)/shard_map/all_gather | solution.py:182
  10.9 307.5 %all-reduce.8.cloned.1.call-start = ((), (), s32[]{:S(2)}) async-start(), calls=%async_computation.9 | async-start | bytes 8388608 | tf_op jit(solution)/shard_map/psum | solution.py:222
  11.0 93.8 %copy-start = (bf16[1024,2048]{1,0:T(8,128)(2,1)S(1)}, bf16[1024,2048]{1,0:T(8,128)(2,1)}, u32[]{:S(2)}) copy-start(bf16[1024,2048]{1,0:T(8,128)(2,1)} %param.27) | copy-start | bytes 12582916
  34.3 73.1 %copy-start.46 = (f32[8,1,256]{2,1,0:T(1,128)}, f32[8,1,256]{2,1,0:T(1,128)S(1)}, u32[]{:S(2)}) copy-start(f32[8,1,256]{2,1,0:T(1,128)S(1)} %convert_element_type.295) | copy-start | bytes 24580
  38.0 71.4 %copy-start.48 = (f32[1024]{0:T(1024)}, f32[1024]{0:T(1024)S(1)}, u32[]{:S(2)}) copy-start(f32[1024]{0:T(1024)S(1)} %get-tuple-element.220) | copy-start | bytes 12292
  71.7 37.7 %copy-start.17 = (bf16[2048,128]{1,0:T(8,128)(2,1)}, bf16[2048,128]{1,0:T(8,128)(2,1)S(1)}, u32[]{:S(2)}) copy-start(bf16[2048,128]{1,0:T(8,128)(2,1)S(1)} %all_gather.25) | copy-start | bytes 1572868
  110.0 5.5 copy-start.25
  110.0 5.5 copy-start.27
  110.1 5.8 copy-start.52
  143.0 9.9 copy-start.9
  143.7 9.3 copy-start.11
  150.2 246.4 %all-gather.13.cloned.1.call-start = ((), (), s32[]{:S(2)}) async-start(), calls=%async_computation.11 | async-start | bytes 9437184 | tf_op jit(solution)/shard_map/all_gather | solution.py:186
  152.9 86.3 %copy-start.53 = (f32[256]{0:T(256)S(1)}, f32[256]{0:T(256)}, u32[]{:S(2)}) copy-start(f32[256]{0:T(256)} %param.35) | copy-start | bytes 3076
  152.9 369.6 %all-gather.11.cloned.1.call-start = ((), (), s32[]{:S(2)}) async-start(), calls=%async_computation.10 | async-start | bytes 9437184 | tf_op jit(solution)/shard_map/all_gather | solution.py:184
  154.1 512.9 %all-reduce.10.cloned.1.call-start = ((), (), s32[]{:S(2)}) async-start(), calls=%async_computation.12 | async-start | bytes 8388608 | tf_op jit(solution)/shard_map/psum | solution.py:256
  159.2 43.2 %collective-permute-start = (bf16[256,2048]{1,0:T(8,128)(2,1)S(1)}, bf16[256,2048]{1,0:T(8,128)(2,1)S(1)}, u32[]{:S(2)}, u32[]{:S(2)}) collective-permute-start(bf16[256,2048]{1,0:T(8,128)(2,1)S(1)} %get-tuple-element.177), channel_id=1, source_target_pairs={{0,4},{4,8},{8,12},{12,16},{16,20},{20,24},{24,28},{28,0},{1,5},{5... | collective-permute-start | bytes 3145736 | tf_op jit(solution)/shard_map/ppermute | solution.py:26
  159.2 45.7 %collective-permute-start.1 = (bf16[256,2048]{1,0:T(8,128)(2,1)S(1)}, bf16[256,2048]{1,0:T(8,128)(2,1)S(1)}, u32[]{:S(2)}, u32[]{:S(2)}) collective-permute-start(bf16[256,2048]{1,0:T(8,128)(2,1)S(1)} %get-tuple-element.177), channel_id=1, source_target_pairs={{0,28},{4,0},{8,4},{12,8},{16,12},{20,16},{24,20},{28,24},{1,29},{... | collective-permute-start | bytes 3145736 | tf_op jit(solution)/shard_map/ppermute | solution.py:31
  202.4 34.3 %collective-permute-start.2 = (bf16[256,2048]{1,0:T(8,128)(2,1)S(1)}, bf16[256,2048]{1,0:T(8,128)(2,1)}, u32[]{:S(2)}, u32[]{:S(2)}) collective-permute-start(bf16[256,2048]{1,0:T(8,128)(2,1)S(1)} %collective-permute-done), channel_id=1, source_target_pairs={{0,4},{4,8},{8,12},{12,16},{16,20},{20,24},{24,28},{28,0},{1,5},{5... | collective-permute-start | bytes 3145736 | tf_op jit(solution)/shard_map/ppermute | solution.py:26
  204.9 85.3 %collective-permute-start.3 = (bf16[256,2048]{1,0:T(8,128)(2,1)S(1)}, bf16[256,2048]{1,0:T(8,128)(2,1)S(1)}, u32[]{:S(2)}, u32[]{:S(2)}) collective-permute-start(bf16[256,2048]{1,0:T(8,128)(2,1)S(1)} %collective-permute-done.1), channel_id=1, source_target_pairs={{0,28},{4,0},{8,4},{12,8},{16,12},{20,16},{24,20},{28,24},{1,29},{... | collective-permute-start | bytes 3145736 | tf_op jit(solution)/shard_map/ppermute | solution.py:31
  236.6 55.9 %collective-permute-start.4 = (bf16[256,2048]{1,0:T(8,128)(2,1)}, bf16[256,2048]{1,0:T(8,128)(2,1)S(1)}, u32[]{:S(2)}, u32[]{:S(2)}) collective-permute-start(bf16[256,2048]{1,0:T(8,128)(2,1)} %collective-permute-done.2), channel_id=1, source_target_pairs={{0,4},{4,8},{8,12},{12,16},{16,20},{20,24},{24,28},{28,0},{1,5},{5... | collective-permute-start | bytes 3145736 | tf_op jit(solution)/shard_map/ppermute | solution.py:26
  290.1 21.4 %collective-permute-start.5 = (bf16[256,2048]{1,0:T(8,128)(2,1)S(1)}, bf16[256,2048]{1,0:T(8,128)(2,1)S(1)}, u32[]{:S(2)}, u32[]{:S(2)}) collective-permute-start(bf16[256,2048]{1,0:T(8,128)(2,1)S(1)} %collective-permute-done.3), channel_id=1, source_target_pairs={{0,28},{4,0},{8,4},{12,8},{16,12},{20,16},{24,20},{28,24},{1,29},{... | collective-permute-start | bytes 3145736 | tf_op jit(solution)/shard_map/ppermute | solution.py:31
  292.5 24.8 %collective-permute-start.6 = (bf16[256,2048]{1,0:T(8,128)(2,1)S(1)}, bf16[256,2048]{1,0:T(8,128)(2,1)S(1)}, u32[]{:S(2)}, u32[]{:S(2)}) collective-permute-start(bf16[256,2048]{1,0:T(8,128)(2,1)S(1)} %collective-permute-done.4), channel_id=1, source_target_pairs={{0,4},{4,8},{8,12},{12,16},{16,20},{20,24},{24,28},{28,0},{1,5},{5... | collective-permute-start | bytes 3145736 | tf_op jit(solution)/shard_map/ppermute | solution.py:26
  318.4 6.0 copy-start.3
  522.5 15.6 copy-start.21
  557.2 13.2 copy-start.61
  583.2 266.4 %reduce-scatter.10.cloned.1.call-start = ((), (), s32[]{:S(2)}) async-start(), calls=%async_computation.14 | async-start | bytes 589824 | tf_op jit(solution)/shard_map/reduce_scatter | solution.py:312
  667.0 8.5 copy-start.2
  667.0 8.5 copy-start.4
  667.0 8.5 copy-start.8
  684.2 75.8 %copy-start.26 = (f32[1024,32]{0,1:T(8,128)S(1)}, f32[1024,32]{0,1:T(8,128)}, u32[]{:S(2)}) copy-start(f32[1024,32]{0,1:T(8,128)} %copy-done.25) | copy-start | bytes 393220
  684.2 75.8 %copy-start.28 = (f32[1024,32]{0,1:T(8,128)S(1)}, f32[1024,32]{0,1:T(8,128)}, u32[]{:S(2)}) copy-start(f32[1024,32]{0,1:T(8,128)} %copy-done.27) | copy-start | bytes 393220
  706.3 8.1 copy-start.30
  706.3 8.1 copy-start.33
  744.0 8.1 copy-start.30
  744.0 8.1 copy-start.33
  765.5 127.5 %reduce-scatter.12.cloned.1.call-start = ((), (), s32[]{:S(2)}) async-start(), calls=%async_computation.15 | async-start | bytes 589824 | tf_op jit(solution)/shard_map/reduce_scatter | solution.py:315
  765.5 14.0 copy-start.35
  765.5 14.4 copy-start.6
  765.5 14.4 copy-start.45
  780.0 6.2 copy-start.20
  782.2 265.7 %all-reduce.12.cloned.1.call-start = ((), (), s32[]{:S(2)}) async-start(), calls=%async_computation.20 | async-start | bytes 16777216 | tf_op jit(solution)/shard_map/psum | solution.py:233
  790.8 6.5 copy-start.59
  790.8 328.7 %reduce-scatter.8.cloned.1.call-start = ((), (), s32[]{:S(2)}) async-start(), calls=%async_computation.13 | async-start | bytes 2359296 | tf_op jit(solution)/shard_map/reduce_scatter | solution.py:309
  797.2 393.8 %reduce-scatter.14.cloned.1.call-start = ((), (), s32[]{:S(2)}) async-start(), calls=%async_computation.16 | async-start | bytes 2359296 | tf_op jit(solution)/shard_map/reduce_scatter | solution.py:318
  804.4 538.2 %reduce-scatter.16.cloned.1.call-start = ((), (), s32[]{:S(2)}) async-start(), calls=%async_computation.17 | async-start | bytes 9437184 | tf_op jit(solution)/shard_map/reduce_scatter | solution.py:324
  818.5 676.1 %reduce-scatter.18.cloned.1.call-start = ((), (), s32[]{:S(2)}) async-start(), calls=%async_computation.18 | async-start | bytes 9437184 | tf_op jit(solution)/shard_map/reduce_scatter | solution.py:327
  832.8 813.7 %reduce-scatter.20.cloned.1.call-start = ((), (), s32[]{:S(2)}) async-start(), calls=%async_computation.19 | async-start | bytes 9437184 | tf_op jit(solution)/shard_map/reduce_scatter | solution.py:330
  847.0 200.8 %copy-start.47 = (f32[8,1,256]{2,1,0:T(1,128)S(1)}, f32[8,1,256]{2,1,0:T(1,128)}, u32[]{:S(2)}) copy-start(f32[8,1,256]{2,1,0:T(1,128)} %copy-done.46) | copy-start | bytes 24580
  847.0 200.8 %copy-start.49 = (f32[1024]{0:T(1024)S(1)}, f32[1024]{0:T(1024)}, u32[]{:S(2)}) copy-start(f32[1024]{0:T(1024)} %copy-done.48) | copy-start | bytes 12292
  847.0 206.4 %copy-start.51 = (bf16[2048]{0:T(1024)(128)(2,1)S(1)}, bf16[2048]{0:T(1024)(128)(2,1)}, u32[]{:S(2)}) copy-start(bf16[2048]{0:T(1024)(128)(2,1)} %get-tuple-element.130) | copy-start | bytes 12292
  847.0 802.6 %copy-start.50 = (f32[1024]{0:T(1024)S(1)}, f32[1024]{0:T(1024)}, u32[]{:S(2)}) copy-start(f32[1024]{0:T(1024)} %get-tuple-element.219) | copy-start | bytes 12292
  1075.8 573.8 %copy-start.54 = (bf16[2048]{0:T(1024)(128)(2,1)}, bf16[2048]{0:T(1024)(128)(2,1)S(1)}, u32[]{:S(2)}) copy-start(bf16[2048]{0:T(1024)(128)(2,1)S(1)} %get-tuple-element.173) | copy-start | bytes 12292
  1075.8 573.8 %copy-start.55 = (bf16[2048]{0:T(1024)(128)(2,1)}, bf16[2048]{0:T(1024)(128)(2,1)S(1)}, u32[]{:S(2)}) copy-start(bf16[2048]{0:T(1024)(128)(2,1)S(1)} %get-tuple-element.172) | copy-start | bytes 12292
  1649.6 57.5 %copy-start.37 = (bf16[256,512]{1,0:T(8,128)(2,1)S(1)}, bf16[256,512]{1,0:T(8,128)(2,1)}, u32[]{:S(2)}) copy-start(bf16[256,512]{1,0:T(8,128)(2,1)} %reduce-scatter.8.cloned.1.call-done) | copy-start | bytes 786436
  1649.6 59.9 %copy-start.40 = (f32[256,128]{1,0:T(8,128)S(1)}, f32[256,128]{1,0:T(8,128)}, u32[]{:S(2)}) copy-start(f32[256,128]{1,0:T(8,128)} %param.32) | copy-start | bytes 393220
  1649.6 65.5 %copy-start.12 = (f32[256,2048]{1,0:T(8,128)S(1)}, f32[256,2048]{1,0:T(8,128)}, u32[]{:S(2)}) copy-start(f32[256,2048]{1,0:T(8,128)} %param.36) | copy-start | bytes 6291460
  1649.6 65.5 %copy-start.22 = (bf16[256,2048]{1,0:T(8,128)(2,1)S(1)}, bf16[256,2048]{1,0:T(8,128)(2,1)}, u32[]{:S(2)}) copy-start(bf16[256,2048]{1,0:T(8,128)(2,1)} %reduce-scatter.16.cloned.1.call-done) | copy-start | bytes 3145732
  1704.1 15.5 copy-start.14
  1704.2 15.5 copy-start.23
  1704.2 15.4 copy-start.31
  1715.1 7.4 copy-start.15
  1715.1 7.4 copy-start.24
  1715.2 7.3 copy-start.32
  (29 other events, 79.6 us)
Sparse Core Ops, SparseCore 0:
  10.7 59.1 all-gather.6
  72.5 52.1 all-gather.8
  150.3 83.0 all-reduce.7
  236.1 160.4 all-gather.12
  399.3 123.1 all-gather.10
  583.3 83.6 all-reduce.9
  765.6 62.0 reduce-scatter.9
  831.9 60.9 reduce-scatter.11
  895.5 152.2 all-reduce.11
  1051.8 67.6 reduce-scatter.7
  1123.6 67.3 reduce-scatter.13
  1194.5 147.9 reduce-scatter.15
  1346.6 148.0 reduce-scatter.17
  1498.1 148.3 reduce-scatter.19
